TPU v7x, 128 devices: a whole 4x4x4 slice. The times are simulated.
128 devices in a mesh: req: 4 (over y), tok: 32 (over z, x, core).
Axes of the slice: x: 4, y: 4, z: 4, core: 2. Of those that a mesh axis runs over, the one named last changes fastest.
Arguments:
- tokens: bfloat16 [8, 2048, 1536], P('req', 'tok'), may hold values from -16 to 16
- gain_attn: float32 [1536], replicated, may hold values from 0.1 to 1.9
- query_weight: bfloat16 [1536, 1536], replicated, may hold values from -0.375 to 0.375
- key_value_weight: bfloat16 [1536, 1024], replicated, may hold values from -0.15625 to 0.15625
- w_out: bfloat16 [1536, 1536], replicated, may hold values from -0.15625 to 0.15625
- kv_pool: bfloat16 [512, 64, 1024], P(('req', 'tok')), may hold values from -170 to 170, as said below
- migrate: int32 [512], P(('req', 'tok')), may hold values from 0 to 511, as said below
- page_table: int32 [8, 64], P('req'), may hold values from 0 to 127, as said below
- cache_len: int32 [8], P('req'), may hold values from 0 to 4096, as said below
- gain_ffn: float32 [1536], replicated, may hold values from 0.1 to 1.9
- routes: int32 [8, 2048, 8], P('req', 'tok'), may hold values from 0 to 31, all different within a row; in each aligned block of 64 rows (0 to 63, 64 to 127, ..., all dimensions but the last counted through in order) at most 24 rows name the same one
- gate_weights: float32 [8, 2048, 8], P('req', 'tok'), may hold values from 0.05 to 0.5
- w_gate_up: bfloat16 [32, 1536, 1024], P('tok'), may hold values from -0.15625 to 0.15625
- w_down: bfloat16 [32, 512, 1536], P('tok'), may hold values from -0.25 to 0.25
Outputs:
- attended: bfloat16 [8, 2048, 1536], P('req', 'tok')
- expert_mix: bfloat16 [8, 2048, 1536], P('req', 'tok')
Inputs may be any that keep to these rules, and one draw needn't show every extreme that they name: `kv_pool`: the values of the cached keys and values. `migrate`: A permutation of all slots that keeps a slot's tok index: slot a*128 + t*4 + i goes to some a2*128 + t*4 + i2. `page_table`: the rows of the 2 requests of one group together hold every slot of the group's pool exactly once. `cache_len`: each length lies within 128 of 0 or of 4096; some request has exactly 4096. `routes`: the 8 experts of a token differ; in each aligned block of 64 rows (one request's tokens on one device) no expert is named more than 24 times.
All inputs are finite; a program needn't handle non-finite values.
Results may differ from a plain program's by a relative error of at most 0.025.
Values may be sent and summed in bfloat16 or wider, within the bound.
No kernel may reach another device: no remote copies, remote signals or barrier semaphores. Data moves between devices by JAX's collectives and lax.ppermute only.
A program may use at most 192 MiB of HBM per device.

v0:
```python
import jax
import jax.numpy as jnp
from jax import lax
from jax.sharding import PartitionSpec as P

QUERY_HEADS = 24
KEY_VALUE_HEADS = 8
HEAD_SIZE = 64
FF = 512
TOPK = 8
MOST = 24
score_masked = -1e30
epsilon = 1e-06
far_position = 1 << 30


def rms_norm(values, gain_vec):
    widened = values.astype(jnp.float32)
    inverse = lax.rsqrt(jnp.mean(widened * widened, axis=-1, keepdims=True) + epsilon)
    return (widened * inverse * gain_vec).astype(jnp.bfloat16)


def pick_block(row_total):
    block_len = min(row_total, 1024)
    while row_total % block_len:
        block_len -= 1
    return block_len


def attend(running, head_rows, meta_abs, query_heads, query_abs):
    row_total = head_rows.shape[1]
    block_len = pick_block(row_total)
    blocks = row_total // block_len
    heads_kv = query_heads.shape[0]
    head_dim = query_heads.shape[2]

    def loop_step(index, carried):
        run_max, run_sum, run_acc = carried
        block = lax.dynamic_slice_in_dim(head_rows, index * block_len, block_len, 1)
        abs_block = lax.dynamic_slice_in_dim(meta_abs, index * block_len, block_len, 0)
        visible = (abs_block[None, :] <= query_abs[:, None])[None, :, :]
        scores = jnp.einsum(
            "hqd,hkd->hqk", query_heads, block[:heads_kv], preferred_element_type=jnp.float32
        ) * head_dim ** (-0.5)
        scores = jnp.where(visible, scores, score_masked)
        new_max = jnp.maximum(run_max, jnp.max(scores, axis=-1))
        weight = jnp.where(visible, jnp.exp(scores - new_max[..., None]), 0.0)
        factor = jnp.exp(run_max - new_max)
        run_sum = run_sum * factor + jnp.sum(weight, axis=-1)
        update = jnp.einsum(
            "hqk,hkd->hqd",
            weight.astype(jnp.bfloat16),
            block[heads_kv:],
            preferred_element_type=jnp.float32,
        )
        run_acc = run_acc * factor[..., None] + update
        return (new_max, run_sum, run_acc)

    return lax.fori_loop(0, blocks, loop_step, running)


def pick_member(state, member_id):
    return jax.tree.map(lambda array: array[member_id], state)


def stack_members(states):
    return jax.tree.map(lambda *arrays: jnp.stack(arrays), *states)


def local(
    tokens,
    gain_attn,
    query_weight,
    key_value_weight,
    w_out,
    kv_pool,
    migrate,
    page_table,
    cache_len,
    gain_ffn,
    routes,
    gate_weights,
    w_gate_up,
    w_down,
):
    request_per_shard, tokens_per_shard, model_width = tokens.shape
    local_rows = request_per_shard * tokens_per_shard
    tok_count = lax.axis_size("tok")
    req_count = lax.axis_size("req")
    tok_index = lax.axis_index("tok")
    kv_width = key_value_weight.shape[1]
    groups_per_head = QUERY_HEADS // KEY_VALUE_HEADS
    flat_rows = tokens.reshape(local_rows, model_width)
    normalized_input = rms_norm(flat_rows, gain_attn)
    query_rows = (
        jnp.dot(normalized_input, query_weight, preferred_element_type=jnp.float32)
        .astype(jnp.bfloat16)
        .reshape(request_per_shard, tokens_per_shard, KEY_VALUE_HEADS, groups_per_head, HEAD_SIZE)
    )
    query_heads = query_rows.transpose(0, 2, 3, 1, 4).reshape(
        request_per_shard, KEY_VALUE_HEADS, groups_per_head * tokens_per_shard, HEAD_SIZE
    )
    keyval_pos = (
        jnp.einsum(
            "rcd,dk->crk",
            normalized_input.reshape(request_per_shard, tokens_per_shard, model_width),
            key_value_weight,
            preferred_element_type=jnp.float32,
        )
        .astype(jnp.bfloat16)
        .reshape(tokens_per_shard, request_per_shard * kv_width)
    )
    span_pos = jnp.arange(tokens_per_shard, dtype=jnp.int32)
    query_abs = cache_len[:, None] + tok_index * tokens_per_shard + span_pos[None, :]
    query_abs_rep = jnp.tile(query_abs, (1, groups_per_head))
    pages_dev = kv_pool.shape[0]
    page_rows = kv_pool.shape[1]
    pages_req = page_table.shape[1]
    slots_all = request_per_shard * pages_req
    cache_pos = jnp.arange(pages_req * page_rows, dtype=jnp.int32)
    target = migrate // slots_all * pages_dev + migrate % pages_dev
    places = jnp.arange(req_count * pages_dev, dtype=jnp.int32)
    route_pages = (places[:, None] == target[None, :]).astype(jnp.bfloat16)
    outgoing = jnp.einsum(
        "sp,prk->srk", route_pages, kv_pool, preferred_element_type=jnp.float32
    ).astype(jnp.bfloat16)
    outgoing = outgoing.reshape(req_count, pages_dev, page_rows, kv_width)
    arrived = lax.all_to_all(outgoing, "req", split_axis=0, concat_axis=0, tiled=True)
    migrated = jnp.sum(arrived, axis=0, dtype=jnp.float32).astype(jnp.bfloat16)
    query_count = groups_per_head * tokens_per_shard
    start_state = (
        jnp.full((request_per_shard, KEY_VALUE_HEADS, query_count), score_masked, jnp.float32),
        jnp.zeros((request_per_shard, KEY_VALUE_HEADS, query_count), jnp.float32),
        jnp.zeros((request_per_shard, KEY_VALUE_HEADS, query_count, HEAD_SIZE), jnp.float32),
    )
    pool_all = lax.all_gather(migrated, "tok", axis=0, tiled=True)
    pool_heads = pool_all.reshape(
        pool_all.shape[0], page_rows, 2 * KEY_VALUE_HEADS, HEAD_SIZE
    ).transpose(2, 0, 1, 3)
    results = []
    for member_id in range(request_per_shard):
        rows = jnp.take(pool_heads, page_table[member_id], axis=1).reshape(
            2 * KEY_VALUE_HEADS, pages_req * page_rows, HEAD_SIZE
        )
        cache_abs = jnp.where(cache_pos < cache_len[member_id], cache_pos, far_position)
        results.append(
            attend(
                pick_member(start_state, member_id),
                rows,
                cache_abs,
                query_heads[member_id],
                query_abs_rep[member_id],
            )
        )
    running = stack_members(results)
    piece = lax.all_gather(keyval_pos, "tok", axis=0, tiled=True)
    row_total = piece.shape[0]
    by_member = piece.reshape(
        row_total, request_per_shard, 2 * KEY_VALUE_HEADS, HEAD_SIZE
    ).transpose(1, 2, 0, 3)
    positions = jnp.arange(row_total, dtype=jnp.int32)
    fold_results = []
    for member_id in range(request_per_shard):
        piece_abs = cache_len[member_id] + positions
        fold_results.append(
            attend(
                pick_member(running, member_id),
                by_member[member_id],
                piece_abs,
                query_heads[member_id],
                query_abs_rep[member_id],
            )
        )
    final_state = stack_members(fold_results)
    run_max, run_sum, run_acc = final_state
    normalized_heads = (
        (run_acc / run_sum[..., None])
        .astype(jnp.bfloat16)
        .reshape(request_per_shard, KEY_VALUE_HEADS, groups_per_head, tokens_per_shard, HEAD_SIZE)
    )
    heads_out = normalized_heads.transpose(0, 3, 1, 2, 4).reshape(
        local_rows, QUERY_HEADS * HEAD_SIZE
    )
    projected = jnp.dot(heads_out, w_out, preferred_element_type=jnp.float32)
    attended = projected.astype(jnp.bfloat16)
    residual = (flat_rows.astype(jnp.float32) + projected).astype(jnp.bfloat16)
    normed_ffn = rms_norm(residual, gain_ffn)
    member = jnp.arange(request_per_shard, dtype=jnp.int32)
    experts_total = tok_count * w_gate_up.shape[0]
    route_local = routes.reshape(request_per_shard, tokens_per_shard * TOPK)
    onehot = route_local[..., None] == jnp.arange(experts_total, dtype=jnp.int32)[None, None, :]
    rank_all = jnp.cumsum(onehot.astype(jnp.int32), axis=1) - 1
    rank_of = jnp.sum(jnp.where(onehot, rank_all, 0), axis=2)
    slot_of = route_local * (request_per_shard * MOST) + member[:, None] * MOST + rank_of
    slot_flat = slot_of.reshape(-1)
    capacity = experts_total * request_per_shard * MOST
    token_ids = jnp.arange(local_rows * TOPK, dtype=jnp.int32) // TOPK
    source = jnp.zeros((capacity,), jnp.int32).at[slot_flat].set(token_ids + 1)
    gathered = jnp.take(normed_ffn, jnp.maximum(source - 1, 0), axis=0)
    outbound = jnp.where((source > 0)[:, None], gathered, jnp.zeros_like(gathered)).reshape(
        experts_total, request_per_shard * MOST, model_width
    )
    inbound = lax.all_to_all(outbound, "tok", split_axis=0, concat_axis=1, tiled=True)
    gate_up = jnp.einsum("erd,edf->erf", inbound, w_gate_up, preferred_element_type=jnp.float32)
    hidden = (jax.nn.silu(gate_up[..., :FF]) * gate_up[..., FF:]).astype(jnp.bfloat16)
    expert_out = jnp.einsum(
        "erf,efd->erd", hidden, w_down, preferred_element_type=jnp.float32
    ).astype(jnp.bfloat16)
    returned = lax.all_to_all(expert_out, "tok", split_axis=1, concat_axis=0, tiled=True)
    picked = jnp.take(returned.reshape(capacity, model_width), slot_flat, axis=0).reshape(
        local_rows, TOPK, model_width
    )
    mixture = jnp.einsum(
        "qk,qkd->qd", gate_weights.reshape(local_rows, TOPK), picked.astype(jnp.float32)
    )
    return (
        attended.reshape(request_per_shard, tokens_per_shard, model_width),
        mixture.astype(jnp.bfloat16).reshape(request_per_shard, tokens_per_shard, model_width),
    )


def solution(mesh):
    placed = (
        P("req", "tok", None),
        P(),
        P(),
        P(),
        P(),
        P(("req", "tok"), None, None),
        P(("req", "tok")),
        P("req", None),
        P("req"),
        P(),
        P("req", "tok", None),
        P("req", "tok", None),
        P("tok", None, None),
        P("tok", None, None),
    )
    return jax.shard_map(
        local,
        mesh=mesh,
        in_specs=placed,
        out_specs=(P("req", "tok", None), P("req", "tok", None)),
        check_vma=False,
    )
```

profile of v0, /device:TPU:0, one launch (start us, length us, event | category | flops | bytes accessed | tf_op | source)
XLA Modules:
  0.0 831.7 jit_solution(13190696790973247134)
XLA Ops:
  21.8 30.8 %all_to_all.23 = bf16[4,4,64,1024]{3,1,2,0:T(4,128)(2,1)} all-to-all(bf16[4,4,64,1024]{3,1,2,0:T(4,128)(2,1)S(1)} %copy.95), channel_id=1, replica_groups=mesh['req'=4,'tok'=32] {'req'}, dimensions={0} | all-to-all | bytes 4194304 | tf_op jit(solution)/shard_map/all_to_all | solution.py:128
  101.6 12.4 %copy.105 = bf16[2048,2048]{0,1:T(8,128)(2,1)} copy(bf16[2048,2048]{1,0:T(8,128)(2,1)} %all-gather.5.cloned.1.call-done) | data formatting | bytes 16777216 | tf_op jit(solution)/shard_map/all_gather | solution.py:156
  114.0 6.4 slice_bitcast_fusion.1
  120.4 21.6 %all-gather.3.cloned.1.call-done = bf16[128,64,1024]{2,1,0:T(8,128)(2,1)} async-done(((bf16[4,64,1024]{2,1,0:T(8,128)(2,1)}), bf16[128,64,1024]{2,1,0:T(8,128)(2,1)}) %all-gather.3.cloned.1.call-update) | async-done | bytes 16777232 | tf_op jit(solution)/shard_map/all_gather | solution.py:136
  142.0 23.0 %copy.98 = bf16[128,64,1024]{0,2,1:T(8,128)(2,1)} copy(bf16[128,64,1024]{2,1,0:T(8,128)(2,1)} %all-gather.3.cloned.1.call-done) | data formatting | bytes 33554432 | tf_op jit(solution)/shard_map/all_gather | solution.py:136
  165.1 46.1 %copy.99 = bf16[128,64,16,64]{3,1,0,2:T(8,128)(2,1)} copy(bf16[128,64,16,64]{0,3,2,1:T(8,128)(2,1)} %bitcast.228) | data formatting | bytes 33554432 | tf_op jit(solution)/shard_map/reshape | solution.py:137
  211.1 11.9 %gather_fusion.2 = bf16[64,16,64,64]{3,2,1,0:T(8,128)(2,1)} fusion(bf16[16,128,64,64]{3,2,1,0:T(8,128)(2,1)} %bitcast.226, s32[1024]{0:T(1024)S(1)} %pad_clamp_fusion.2), kind=kCustom, calls=%fused_computation.clone | custom fusion | bytes 16777472 | tf_op jit(solution)/shard_map/jit(_take)/gather | solution.py:142
  223.0 11.9 %gather_fusion.3 = bf16[64,16,64,64]{3,2,1,0:T(8,128)(2,1)} fusion(bf16[16,128,64,64]{3,2,1,0:T(8,128)(2,1)} %bitcast.227, s32[1024]{0:T(1024)S(1)} %pad_clamp_fusion.1), kind=kCustom, calls=%fused_computation.1.clone | custom fusion | bytes 16777472 | tf_op jit(solution)/shard_map/jit(_take)/gather | solution.py:142
  234.9 23.0 %select_bitcast_fusion = (bf16[16,64,64,64]{3,2,0,1:T(8,128)(2,1)}, bf16[16,64,64,64]{3,2,0,1:T(8,128)(2,1)}) fusion(bf16[64,16,64,64]{3,2,1,0:T(8,128)(2,1)} %gather_fusion.3, pred[64]{0:T(512)(128)(4,1)S(1)} %get-tuple-element.895, bf16[64,16,64,64]{3,2,1,0:T(8,128)(2,1)} %gather_fusion.2, pred[64]{0:T(512)(128)(4,1)S(1)} %get-tuple-element.873), kind=kLoop, calls=%fused_computation.91 | loop fusion | flops 8388608 | bytes 33554560 | tf_op jit(solution)/shard_map/jit(_take)/select_n | solution.py:142
  257.9 22.9 %copy.100 = bf16[16,64,64,64]{2,1,3,0:T(8,128)(2,1)} copy(bf16[16,64,64,64]{3,2,0,1:T(8,128)(2,1)} %get-tuple-element.902) | data formatting | bytes 16777216 | tf_op jit(solution)/shard_map/jit(_take)/select_n | solution.py:142
  280.7 22.6 %reshape.410 = bf16[16,4096,64]{1,2,0:T(8,128)(2,1)} reshape(bf16[16,64,64,64]{2,1,3,0:T(8,128)(2,1)} %copy.100) | data formatting | bytes 16777216 | tf_op jit(solution)/shard_map/reshape | solution.py:142
  303.3 60.5 %while.74 = (s32[]{:T(128)}, f32[8,192]{1,0:T(8,128)S(1)}, f32[8,192]{1,0:T(8,128)S(1)}, f32[8,192,64]{1,2,0:T(8,128)}, s32[4096]{0:T(1024)S(1)}, /*index=5*/bf1...) while((s32[]{:T(128)}, f32[8,192]{1,0:T(8,128)S(1)}, ...), condition=%wide.region_5.7_spmd.clone, body=%wide.region_2.6_spmd.clone.sunk | while | flops 423599616 | bytes 24100308 | solution.py:59
  327.8 5.7 fusion.181
  343.0 5.7 fusion.181
  358.1 5.7 fusion.181
  363.9 27.0 %while.72 = (s32[]{:T(128)}, f32[8,192]{1,0:T(8,128)S(1)}, f32[8,192]{1,0:T(8,128)S(1)}, f32[8,192,64]{1,2,0:T(8,128)}, s32[2048]{0:T(1024)S(1)}, /*index=5*/bf1...) while((s32[]{:T(128)}, f32[8,192]{1,0:T(8,128)S(1)}, ...), condition=%wide.region_9.11_spmd.clone, body=%wide.region_6.10_spmd.clone.sunk | while | flops 423496704 | bytes 49266148 | solution.py:59
  391.5 22.9 %copy.108 = bf16[16,64,64,64]{2,1,3,0:T(8,128)(2,1)} copy(bf16[16,64,64,64]{3,2,0,1:T(8,128)(2,1)} %get-tuple-element.901) | data formatting | bytes 16777216 | tf_op jit(solution)/shard_map/jit(_take)/select_n | solution.py:142
  414.4 22.6 %reshape.414 = bf16[16,4096,64]{1,2,0:T(8,128)(2,1)} reshape(bf16[16,64,64,64]{2,1,3,0:T(8,128)(2,1)} %copy.108) | data formatting | bytes 16777216 | tf_op jit(solution)/shard_map/reshape | solution.py:142
  437.0 63.0 %while.75 = (s32[]{:T(128)}, f32[8,192]{1,0:T(8,128)S(1)}, f32[8,192]{1,0:T(8,128)S(1)}, f32[8,192,64]{1,2,0:T(8,128)}, s32[4096]{0:T(1024)}, /*index=5*/bf16[16...) while((s32[]{:T(128)}, f32[8,192]{1,0:T(8,128)S(1)}, ...), condition=%wide.region_13.15_spmd.clone, body=%wide.region_10.14_spmd.clone.sunk | while | flops 423599616 | bytes 24100308 | solution.py:59
  462.7 5.7 fusion.188
  478.5 5.7 fusion.188
  494.3 5.7 fusion.188
  500.0 27.1 %while.73 = (s32[]{:T(128)}, f32[8,192]{1,0:T(8,128)S(1)}, f32[8,192]{1,0:T(8,128)S(1)}, f32[8,192,64]{1,2,0:T(8,128)}, s32[2048]{0:T(1024)S(1)}, /*index=5*/bf1...) while((s32[]{:T(128)}, f32[8,192]{1,0:T(8,128)S(1)}, ...), condition=%wide.region_17.19_spmd.clone, body=%wide.region_14.18_spmd.clone.sunk | while | flops 423496704 | bytes 49266148 | solution.py:59
  545.9 6.2 gather_fusion
  554.9 62.1 %all_to_all.24 = bf16[32,48,1536]{2,1,0:T(8,128)(2,1)S(1)} all-to-all(bf16[32,48,1536]{2,1,0:T(8,128)(2,1)S(1)} %select_select_fusion), channel_id=1, replica_groups=mesh['req'=4,'tok'=32] {'tok'}, dimensions={0} | all-to-all | bytes 9437184 | tf_op jit(solution)/shard_map/all_to_all | solution.py:203
  625.3 52.2 %copy.141 = bf16[1,1536,1536]{2,0,1:T(2,128)(2,1)} copy(bf16[1,1536,1536]{2,1,0:T(8,128)(2,1)S(1)} %fusion.78) | data formatting | bytes 9437184 | tf_op jit(solution)/shard_map/convert_element_type | solution.py:208
  678.1 32.0 %reduce.4 = bf16[1536,1536]{1,0:T(8,128)(2,1)} reduce(bf16[1536,1,1536]{2,1,0:T(2,128)(2,1)} %bitcast.229, bf16[]{:T(256)} %broadcast.485), dimensions={1}, to_apply=%bitcast.192.reduce_sub_computation | reduce | bytes 9437186
  710.0 8.2 reshape.485
  724.2 59.0 %all-to-all-done.2 = bf16[32,2,36864]{2,1,0:T(2,128)(2,1)} async-done(((bf16[32,2,36864]{2,1,0:T(2,128)(2,1)}), bf16[32,2,36864]{2,1,0:T(2,128)(2,1)}, u32[]{:S(2)}, u32[]{:S(2)}) %all-to-all-start.2) | async-done | bytes 4718624 | tf_op jit(solution)/shard_map/all_to_all | solution.py:209
  783.2 20.2 %reshape.486 = bf16[1536,1,1536]{2,1,0:T(2,128)(2,1)} reshape(bf16[32,2,36864]{2,1,0:T(2,128)(2,1)} %all-to-all-done.2) | data formatting | bytes 9437184
  803.4 7.2 copy.139
  810.7 10.2 %gather_fusion.1 = bf16[1024,1536]{1,0:T(8,128)(2,1)} fusion(bf16[1536,1536]{1,0:T(8,128)(2,1)} %bitcast.225, s32[1024]{0:T(1024)S(1)} %broadcast_clamp_fusion), kind=kCustom, calls=%fused_computation.3 | custom fusion | bytes 6295552 | tf_op jit(solution)/shard_map/jit(_take)/gather | solution.py:210
  (262 shorter events, 246.4 us)
Async XLA Ops:
  7.2 609.8 %copy-start = (bf16[1,1536,1024]{2,1,0:T(8,128)(2,1)S(1)}, bf16[1,1536,1024]{2,1,0:T(8,128)(2,1)}, u32[]{:S(2)}) copy-start(bf16[1,1536,1024]{2,1,0:T(8,128)(2,1)} %param.36) | copy-start | bytes 9437188
  7.2 4.8 copy-start.24
  7.2 94.4 %all-gather.5.cloned.1.call-start = ((), (), s32[]{:S(2)}) async-start(), calls=%async_computation.4 | async-start | bytes 8650752 | tf_op jit(solution)/shard_map/all_gather | solution.py:156
  12.0 130.0 %all-gather.3.cloned.1.call-start = ((), (), s32[]{:S(2)}) async-start(), calls=%async_computation.3 | async-start | bytes 17301504 | tf_op jit(solution)/shard_map/all_gather | solution.py:136
  19.4 44.1 %copy-start.3 = (bf16[2,64,1536]{2,1,0:T(8,128)(2,1)S(1)}, bf16[2,64,1536]{2,1,0:T(8,128)(2,1)}, u32[]{:S(2)}) copy-start(bf16[2,64,1536]{2,1,0:T(8,128)(2,1)} %param.24) | copy-start | bytes 1179652
  86.4 27.6 %copy-start.12 = (s32[2,512]{1,0:T(2,128)}, s32[2,512]{1,0:T(2,128)S(1)}, u32[]{:S(2)}) copy-start(s32[2,512]{1,0:T(2,128)S(1)} %fusion.111) | copy-start | bytes 12292
  87.2 26.9 %copy-start.9 = (s32[2,64,8]{1,2,0:T(8,128)}, s32[2,64,8]{1,2,0:T(8,128)S(1)}, u32[]{:S(2)}) copy-start(s32[2,64,8]{1,2,0:T(8,128)S(1)} %broadcast_multiply_fusion) | copy-start | bytes 12292
  87.4 0.6 copy-start.21
  88.0 26.0 %copy-start.17 = (s32[1024,1]{0,1:T(1,128)}, s32[1024,1]{0,1:T(1,128)S(1)}, u32[]{:S(2)}) copy-start(s32[1024,1]{0,1:T(1,128)S(1)} %compare_select_fusion) | copy-start | bytes 12292
  367.0 2.7 copy-start.1
  380.4 2.7 copy-start.1
  414.4 22.6 %copy-start.6 = (f32[8,192]{1,0:T(8,128)S(1)}, f32[8,192]{1,0:T(8,128)}, u32[]{:S(2)}) copy-start(f32[8,192]{1,0:T(8,128)} %custom-call.3) | copy-start | bytes 18436
  414.4 22.6 %copy-start.7 = (f32[8,192]{1,0:T(8,128)S(1)}, f32[8,192]{1,0:T(8,128)}, u32[]{:S(2)}) copy-start(f32[8,192]{1,0:T(8,128)} %custom-call.4) | copy-start | bytes 18436
  414.4 22.6 %copy-start.11 = (s32[64]{0:T(128)S(1)}, s32[64]{0:T(128)}, u32[]{:S(2)}) copy-start(s32[64]{0:T(128)} %get-tuple-element.1177) | copy-start | bytes 772
  437.0 63.0 %copy-start.8 = (s32[2048]{0:T(1024)S(1)}, s32[2048]{0:T(1024)}, u32[]{:S(2)}) copy-start(s32[2048]{0:T(1024)} %iota_add_fusion) | copy-start | bytes 24580
  503.3 2.7 copy-start.2
  516.7 2.7 copy-start.2
  527.1 14.4 %copy-start.4 = (bf16[2,64,1536]{2,1,0:T(8,128)(2,1)S(1)}, bf16[2,64,1536]{2,1,0:T(8,128)(2,1)}, u32[]{:S(2)}) copy-start(bf16[2,64,1536]{2,1,0:T(8,128)(2,1)} %param.24) | copy-start | bytes 1179652
  530.0 15.0 %copy-start.19 = (f32[1536]{0:T(1024)S(1)}, f32[1536]{0:T(1024)}, u32[]{:S(2)}) copy-start(f32[1536]{0:T(1024)} %param.33) | copy-start | bytes 18436
  533.0 12.9 %copy-start.14 = (s32[2048]{0:T(1024)S(1)}, s32[2048]{0:T(1024)}, u32[]{:S(2)}) copy-start(s32[2048]{0:T(1024)} %pad_clamp_fusion) | copy-start | bytes 24580
  541.6 3.4 copy-start.5
  545.9 6.2 copy-start.15
  545.9 6.2 copy-start.16
  617.0 5.4 copy-start.23
  718.3 5.2 copy-start.13
  718.3 5.4 copy-start.10
  718.3 5.5 copy-start.22
  718.3 5.8 copy-start.20
  718.3 5.9 copy-start.18
  718.3 64.9 %all-to-all-start.2 = ((bf16[32,2,36864]{2,1,0:T(2,128)(2,1)}), bf16[32,2,36864]{2,1,0:T(2,128)(2,1)}, u32[]{:S(2)}, u32[]{:S(2)}) async-start(bf16[32,2,36864]{2,1,0:T(2,128)(2,1)} %reshape.485), calls=%async_computation.2 | async-start | bytes 9437184 | tf_op jit(solution)/shard_map/all_to_all | solution.py:209
Sparse Core Ops, SparseCore 0:
  12.1 55.4 all-gather.4
  69.9 72.0 all-gather.2
where the time goes:
time: 845 us; the launch traced here: 832 us
  local copies, waits for them, and re-layouts  372 us (44%)
  matrix products  145 us (17%)
  other arithmetic  120 us (14%)
  blocking collectives  92.9 us (11%)
  waiting for transfers between devices  80.6 us (10%)
  between operations  14.7 us (2%)
    dot_general x12, matrix products, loop_step(): jnp.einsum('hqk,hkd->hqd', weight.astype(jnp.bfloat16), block[heads_kv:],...  68.1 us
    all_to_all x1, blocking collectives, local(): lax.all_to_all(outbound, 'tok', split_axis=0, concat_axis=1, tiled=True)  62.1 us
    all_to_all x1, waiting for transfers between devices, local(): lax.all_to_all(expert_out, 'tok', split_axis=1, concat_axis=0, tiled=True)  59 us
    convert_element_type x1, local copies, waits for them, and re-layouts, local(): expert_out = jnp.einsum('erf,efd->erd', hidden, w_down, preferred_element...  52.2 us
    dot_general x12, matrix products, loop_step(): jnp.einsum('hqd,hkd->hqk', query_heads, block[:heads_kv], preferred_eleme...  52.2 us
    reshape x1, local copies, waits for them, and re-layouts, local(): pool_all.reshape(pool_all.shape[0], page_rows, 2 * KEY_VALUE_HEADS, HEAD_...  46.1 us
    select_n x2, local copies, waits for them, and re-layouts, local(): jnp.take(pool_heads, page_table[member_id], axis=1)  45.8 us
    reshape x2, local copies, waits for them, and re-layouts, local(): jnp.take(pool_heads, page_table[member_id], axis=1)  45.2 us
  transfers between devices with their start and end apart: 3, of which 2 were waited for; matrix products, arithmetic and copies ran while one was open for 9% of the time, Pallas kernels for 0%

commit v1 on v0

--- a/solution.py
+++ b/solution.py
@@ -206,7 +206,10 @@
     expert_out = jnp.einsum(
         "erf,efd->erd", hidden, w_down, preferred_element_type=jnp.float32
     ).astype(jnp.bfloat16)
-    returned = lax.all_to_all(expert_out, "tok", split_axis=1, concat_axis=0, tiled=True)
+    returned = jnp.concatenate(
+        lax.all_to_all(jnp.stack(jnp.split(expert_out, lax.axis_size("tok"), axis=1)), "tok", 0, 0),
+        axis=0,
+    )
     picked = jnp.take(returned.reshape(capacity, model_width), slot_flat, axis=0).reshape(
         local_rows, TOPK, model_width
     )

time: 845 us -> 745 us (0.88)
  local copies, waits for them, and re-layouts: 372 us -> 305 us
  other arithmetic: 120 us -> 88.3 us
    convert_element_type x1 -> x0, local copies, waits for them, and re-layouts: 52.2 us -> none  [local(): expert_out = jnp.einsum('erf,efd->erd', hidden, w_down, preferred_element...]
    unnamed x7 -> x6, other arithmetic: 32 us -> 0.01 us
    unnamed x56 -> x83, local copies, waits for them, and re-layouts: 40.1 us -> 24.7 us
  transfers between devices with their start and end apart: 3 -> 3, of which waited for: 2 -> 2; matrix products, arithmetic and copies ran while one was open for 9% -> 11% of each run, Pallas kernels for 0% -> 0%
where the time goes in v1:
time: 745 us; the launch traced here: 732 us
  local copies, waits for them, and re-layouts  305 us (41%)
  matrix products  145 us (19%)
  blocking collectives  93 us (12%)
  other arithmetic  88.3 us (12%)
  waiting for transfers between devices  80.5 us (11%)
  between operations  14.6 us (2%)
    dot_general x12, matrix products, loop_step(): jnp.einsum('hqk,hkd->hqd', weight.astype(jnp.bfloat16), block[heads_kv:],...  68.1 us
    all_to_all x1, blocking collectives, local(): lax.all_to_all(outbound, 'tok', split_axis=0, concat_axis=1, tiled=True)  62.1 us
    all_to_all x1, waiting for transfers between devices, local(): lax.all_to_all(jnp.stack(jnp.split(expert_out, lax.axis_size('tok'), axis...  59 us
    dot_general x12, matrix products, loop_step(): jnp.einsum('hqd,hkd->hqk', query_heads, block[:heads_kv], preferred_eleme...  52.2 us
    reshape x1, local copies, waits for them, and re-layouts, local(): pool_all.reshape(pool_all.shape[0], page_rows, 2 * KEY_VALUE_HEADS, HEAD_...  46.1 us
    select_n x2, local copies, waits for them, and re-layouts, local(): jnp.take(pool_heads, page_table[member_id], axis=1)  45.7 us
    reshape x2, local copies, waits for them, and re-layouts, local(): jnp.take(pool_heads, page_table[member_id], axis=1)  45.1 us
    reduce_sum x12, other arithmetic, loop_step(): run_sum = run_sum * factor + jnp.sum(weight, axis=-1)  39.6 us
  transfers between devices with their start and end apart: 3, of which 2 were waited for; matrix products, arithmetic and copies ran while one was open for 11% of the time, Pallas kernels for 0%

profile of v1, /device:TPU:0, one launch (start us, length us, event | category | flops | bytes accessed | tf_op | source)
XLA Modules:
  0.0 732.3 jit_solution(8099548670011313187)
XLA Ops:
  21.8 30.9 %all_to_all.19 = bf16[4,4,64,1024]{3,1,2,0:T(4,128)(2,1)} all-to-all(bf16[4,4,64,1024]{3,1,2,0:T(4,128)(2,1)S(1)} %copy.66), channel_id=1, replica_groups=mesh['req'=4,'tok'=32] {'req'}, dimensions={0} | all-to-all | bytes 4194304 | tf_op jit(solution)/shard_map/all_to_all | solution.py:128
  101.7 12.5 %copy.76 = bf16[2048,2048]{0,1:T(8,128)(2,1)} copy(bf16[2048,2048]{1,0:T(8,128)(2,1)} %all-gather.5.cloned.1.call-done) | data formatting | bytes 16777216 | tf_op jit(solution)/shard_map/all_gather | solution.py:156
  114.2 6.4 slice_bitcast_fusion.1
  120.6 21.4 %all-gather.3.cloned.1.call-done = bf16[128,64,1024]{2,1,0:T(8,128)(2,1)} async-done(((bf16[4,64,1024]{2,1,0:T(8,128)(2,1)}), bf16[128,64,1024]{2,1,0:T(8,128)(2,1)}) %all-gather.3.cloned.1.call-update) | async-done | bytes 16777232 | tf_op jit(solution)/shard_map/all_gather | solution.py:136
  142.0 23.0 %copy.69 = bf16[128,64,1024]{0,2,1:T(8,128)(2,1)} copy(bf16[128,64,1024]{2,1,0:T(8,128)(2,1)} %all-gather.3.cloned.1.call-done) | data formatting | bytes 33554432 | tf_op jit(solution)/shard_map/all_gather | solution.py:136
  165.0 46.1 %copy.70 = bf16[128,64,16,64]{3,1,0,2:T(8,128)(2,1)} copy(bf16[128,64,16,64]{0,3,2,1:T(8,128)(2,1)} %bitcast.349) | data formatting | bytes 33554432 | tf_op jit(solution)/shard_map/reshape | solution.py:137
  211.0 11.9 %gather_fusion.2 = bf16[64,16,64,64]{3,2,1,0:T(8,128)(2,1)} fusion(bf16[16,128,64,64]{3,2,1,0:T(8,128)(2,1)} %bitcast.347, s32[1024]{0:T(1024)S(1)} %pad_clamp_fusion.2), kind=kCustom, calls=%fused_computation.clone | custom fusion | bytes 16777472 | tf_op jit(solution)/shard_map/jit(_take)/gather | solution.py:142
  222.9 11.9 %gather_fusion.3 = bf16[64,16,64,64]{3,2,1,0:T(8,128)(2,1)} fusion(bf16[16,128,64,64]{3,2,1,0:T(8,128)(2,1)} %bitcast.348, s32[1024]{0:T(1024)S(1)} %pad_clamp_fusion.1), kind=kCustom, calls=%fused_computation.1.clone | custom fusion | bytes 16777472 | tf_op jit(solution)/shard_map/jit(_take)/gather | solution.py:142
  234.8 23.0 %select_bitcast_fusion = (bf16[16,64,64,64]{3,2,0,1:T(8,128)(2,1)}, bf16[16,64,64,64]{3,2,0,1:T(8,128)(2,1)}) fusion(bf16[64,16,64,64]{3,2,1,0:T(8,128)(2,1)} %gather_fusion.3, pred[64]{0:T(512)(128)(4,1)S(1)} %get-tuple-element.863, bf16[64,16,64,64]{3,2,1,0:T(8,128)(2,1)} %gather_fusion.2, pred[64]{0:T(512)(128)(4,1)S(1)} %get-tuple-element.841), kind=kLoop, calls=%fused_computation.91 | loop fusion | flops 8388608 | bytes 33554560 | tf_op jit(solution)/shard_map/jit(_take)/select_n | solution.py:142
  257.8 22.9 %copy.71 = bf16[16,64,64,64]{2,1,3,0:T(8,128)(2,1)} copy(bf16[16,64,64,64]{3,2,0,1:T(8,128)(2,1)} %get-tuple-element.870) | data formatting | bytes 16777216 | tf_op jit(solution)/shard_map/jit(_take)/select_n | solution.py:142
  280.6 22.6 %reshape.403 = bf16[16,4096,64]{1,2,0:T(8,128)(2,1)} reshape(bf16[16,64,64,64]{2,1,3,0:T(8,128)(2,1)} %copy.71) | data formatting | bytes 16777216 | tf_op jit(solution)/shard_map/reshape | solution.py:142
  303.2 60.4 %while.74 = (s32[]{:T(128)}, f32[8,192]{1,0:T(8,128)S(1)}, f32[8,192]{1,0:T(8,128)S(1)}, f32[8,192,64]{1,2,0:T(8,128)}, s32[4096]{0:T(1024)S(1)}, /*index=5*/bf1...) while((s32[]{:T(128)}, f32[8,192]{1,0:T(8,128)S(1)}, ...), condition=%wide.region_5.7_spmd.clone, body=%wide.region_2.6_spmd.clone.sunk | while | flops 423599616 | bytes 24100308 | solution.py:59
  327.6 5.7 fusion.213
  342.8 5.7 fusion.213
  357.9 5.7 fusion.213
  363.6 27.0 %while.72 = (s32[]{:T(128)}, f32[8,192]{1,0:T(8,128)S(1)}, f32[8,192]{1,0:T(8,128)S(1)}, f32[8,192,64]{1,2,0:T(8,128)}, s32[2048]{0:T(1024)S(1)}, /*index=5*/bf1...) while((s32[]{:T(128)}, f32[8,192]{1,0:T(8,128)S(1)}, ...), condition=%wide.region_9.11_spmd.clone, body=%wide.region_6.10_spmd.clone.sunk | while | flops 423496704 | bytes 49266148 | solution.py:59
  371.5 5.7 fusion.200
  384.9 5.7 fusion.200
  391.3 22.9 %copy.79 = bf16[16,64,64,64]{2,1,3,0:T(8,128)(2,1)} copy(bf16[16,64,64,64]{3,2,0,1:T(8,128)(2,1)} %get-tuple-element.869) | data formatting | bytes 16777216 | tf_op jit(solution)/shard_map/jit(_take)/select_n | solution.py:142
  414.1 22.6 %reshape.407 = bf16[16,4096,64]{1,2,0:T(8,128)(2,1)} reshape(bf16[16,64,64,64]{2,1,3,0:T(8,128)(2,1)} %copy.79) | data formatting | bytes 16777216 | tf_op jit(solution)/shard_map/reshape | solution.py:142
  436.8 63.1 %while.75 = (s32[]{:T(128)}, f32[8,192]{1,0:T(8,128)S(1)}, f32[8,192]{1,0:T(8,128)S(1)}, f32[8,192,64]{1,2,0:T(8,128)}, s32[4096]{0:T(1024)}, /*index=5*/bf16[16...) while((s32[]{:T(128)}, f32[8,192]{1,0:T(8,128)S(1)}, ...), condition=%wide.region_13.15_spmd.clone, body=%wide.region_10.14_spmd.clone.sunk | while | flops 423599616 | bytes 24100308 | solution.py:59
  446.9 5.6 fusion.220
  462.5 5.7 fusion.220
  478.3 5.7 fusion.220
  494.1 5.7 fusion.220
  499.8 27.2 %while.73 = (s32[]{:T(128)}, f32[8,192]{1,0:T(8,128)S(1)}, f32[8,192]{1,0:T(8,128)S(1)}, f32[8,192,64]{1,2,0:T(8,128)}, s32[2048]{0:T(1024)S(1)}, /*index=5*/bf1...) while((s32[]{:T(128)}, f32[8,192]{1,0:T(8,128)S(1)}, ...), condition=%wide.region_17.19_spmd.clone, body=%wide.region_14.18_spmd.clone.sunk | while | flops 423496704 | bytes 49266148 | solution.py:59
  507.9 5.7 fusion.206
  521.3 5.7 fusion.206
  545.8 6.2 gather_fusion
  554.7 62.1 %all_to_all.20 = bf16[32,48,1536]{2,1,0:T(8,128)(2,1)S(1)} all-to-all(bf16[32,48,1536]{2,1,0:T(8,128)(2,1)S(1)} %select_select_fusion), channel_id=1, replica_groups=mesh['req'=4,'tok'=32] {'tok'}, dimensions={0} | all-to-all | bytes 9437184 | tf_op jit(solution)/shard_map/all_to_all | solution.py:203
  652.3 59.0 %all-to-all-done.2 = bf16[32,1,48,1536]{3,2,1,0:T(8,128)(2,1)} async-done(((bf16[32,1,48,1536]{3,2,1,0:T(8,128)(2,1)}), bf16[32,1,48,1536]{3,2,1,0:T(8,128)(2,1)}, u32[]{:S(2)}, u32[]{:S(2)}) %all-to-all-start.2) | async-done | bytes 4718624 | tf_op jit(solution)/shard_map/all_to_all | solution.py:210
  711.4 10.2 %gather_fusion.1 = bf16[1024,1536]{1,0:T(8,128)(2,1)} fusion(bf16[1536,1536]{1,0:T(8,128)(2,1)} %bitcast.67, s32[1024]{0:T(1024)S(1)} %broadcast_clamp_fusion), kind=kCustom, calls=%fused_computation.3 | custom fusion | bytes 6295552 | tf_op jit(solution)/shard_map/jit(_take)/gather | solution.py:213
  (288 shorter events, 238.7 us)
Async XLA Ops:
  7.2 609.7 %copy-start = (bf16[1,1536,1024]{2,1,0:T(8,128)(2,1)S(1)}, bf16[1,1536,1024]{2,1,0:T(8,128)(2,1)}, u32[]{:S(2)}) copy-start(bf16[1,1536,1024]{2,1,0:T(8,128)(2,1)} %param.36) | copy-start | bytes 9437188
  7.2 4.8 copy-start.24
  7.2 94.5 %all-gather.5.cloned.1.call-start = ((), (), s32[]{:S(2)}) async-start(), calls=%async_computation.4 | async-start | bytes 8650752 | tf_op jit(solution)/shard_map/all_gather | solution.py:156
  12.0 130.0 %all-gather.3.cloned.1.call-start = ((), (), s32[]{:S(2)}) async-start(), calls=%async_computation.3 | async-start | bytes 17301504 | tf_op jit(solution)/shard_map/all_gather | solution.py:136
  21.8 41.8 %copy-start.3 = (bf16[2,64,1536]{2,1,0:T(8,128)(2,1)S(1)}, bf16[2,64,1536]{2,1,0:T(8,128)(2,1)}, u32[]{:S(2)}) copy-start(bf16[2,64,1536]{2,1,0:T(8,128)(2,1)} %param.24) | copy-start | bytes 1179652
  86.5 27.6 %copy-start.12 = (s32[2,512]{1,0:T(2,128)}, s32[2,512]{1,0:T(2,128)S(1)}, u32[]{:S(2)}) copy-start(s32[2,512]{1,0:T(2,128)S(1)} %fusion.143) | copy-start | bytes 12292
  87.3 26.9 %copy-start.9 = (s32[2,64,8]{1,2,0:T(8,128)}, s32[2,64,8]{1,2,0:T(8,128)S(1)}, u32[]{:S(2)}) copy-start(s32[2,64,8]{1,2,0:T(8,128)S(1)} %broadcast_multiply_fusion) | copy-start | bytes 12292
  87.5 0.6 copy-start.21
  88.2 26.0 %copy-start.17 = (s32[1024,1]{0,1:T(1,128)}, s32[1024,1]{0,1:T(1,128)S(1)}, u32[]{:S(2)}) copy-start(s32[1024,1]{0,1:T(1,128)S(1)} %compare_select_fusion) | copy-start | bytes 12292
  366.8 2.7 copy-start.1
  380.1 2.7 copy-start.1
  414.1 22.6 %copy-start.6 = (f32[8,192]{1,0:T(8,128)S(1)}, f32[8,192]{1,0:T(8,128)}, u32[]{:S(2)}) copy-start(f32[8,192]{1,0:T(8,128)} %custom-call.3) | copy-start | bytes 18436
  414.1 22.6 %copy-start.7 = (f32[8,192]{1,0:T(8,128)S(1)}, f32[8,192]{1,0:T(8,128)}, u32[]{:S(2)}) copy-start(f32[8,192]{1,0:T(8,128)} %custom-call.4) | copy-start | bytes 18436
  414.1 22.6 %copy-start.11 = (s32[64]{0:T(128)S(1)}, s32[64]{0:T(128)}, u32[]{:S(2)}) copy-start(s32[64]{0:T(128)} %get-tuple-element.1145) | copy-start | bytes 772
  436.7 63.1 %copy-start.8 = (s32[2048]{0:T(1024)S(1)}, s32[2048]{0:T(1024)}, u32[]{:S(2)}) copy-start(s32[2048]{0:T(1024)} %iota_add_fusion) | copy-start | bytes 24580
  503.1 2.7 copy-start.2
  516.5 2.7 copy-start.2
  527.0 14.4 %copy-start.4 = (bf16[2,64,1536]{2,1,0:T(8,128)(2,1)S(1)}, bf16[2,64,1536]{2,1,0:T(8,128)(2,1)}, u32[]{:S(2)}) copy-start(bf16[2,64,1536]{2,1,0:T(8,128)(2,1)} %param.24) | copy-start | bytes 1179652
  535.6 9.2 %copy-start.19 = (f32[1536]{0:T(1024)S(1)}, f32[1536]{0:T(1024)}, u32[]{:S(2)}) copy-start(f32[1536]{0:T(1024)} %param.33) | copy-start | bytes 18436
  538.6 7.1 copy-start.14
  541.4 3.4 copy-start.5
  545.8 6.2 copy-start.15
  545.8 6.2 copy-start.16
  616.8 5.4 copy-start.23
  646.6 5.0 copy-start.13
  646.6 5.1 copy-start.10
  646.6 5.3 copy-start.22
  646.6 5.6 copy-start.20
  646.6 5.7 copy-start.18
  646.6 64.8 %all-to-all-start.2 = ((bf16[32,1,48,1536]{3,2,1,0:T(8,128)(2,1)}), bf16[32,1,48,1536]{3,2,1,0:T(8,128)(2,1)}, u32[]{:S(2)}, u32[]{:S(2)}) async-start(bf16[32,1,48,1536]{3,2,1,0:T(8,128)(2,1)} %fusion.110), calls=%async_computation.2 | async-start | bytes 9437184 | tf_op jit(solution)/shard_map/all_to_all | solution.py:210
Sparse Core Ops, SparseCore 0:
  12.1 55.4 all-gather.4
  69.9 72.0 all-gather.2
